TPU v7x, 32 devices: a whole 2x2x4 slice. The times are simulated.
32 devices in a mesh: blk: 8 (over y, x, core), col: 4 (over z).
Axes of the slice: x: 2, y: 2, z: 4, core: 2. Of those that a mesh axis runs over, the one named last changes fastest.
Arguments:
- documents: bfloat16 [6144, 768], P('blk'), may hold values from -6 to 6
- landmarks: bfloat16 [4096, 768], P(('blk', 'col')), may hold values from -6 to 6
- eigen_vectors: bfloat16 [4096, 256], P(('blk', 'col')), may hold values from -6 to 6
- land_degree: float32 [4096], P(('blk', 'col')), may hold values from 0.5 to 8
- eigen_values: float32 [256], replicated, may hold values from 0.005 to 0.05
- tile_mask: int32 [48, 32], P('blk'), may hold values from 0 to 1, as said below
- labels: int32 [6144], P(('blk', 'col')), may hold values from 0 to 999
Outputs:
- embedding: float32 [6144, 256], P(('blk', 'col'))
- centroids: float32 [1000, 256], replicated
Inputs may be any that keep to these rules, and one draw needn't show every extreme that they name: `tile_mask`: 1 marks a live tile of 128 documents by 128 landmarks; every document block has at least one live tile.
All inputs are finite; a program needn't handle non-finite values.
Results may differ from a plain program's by a relative error of at most 0.0041.
Values may be sent and summed in bfloat16 or wider, within the bound.
No kernel may reach another device: no remote copies, remote signals or barrier semaphores. Data moves between devices by JAX's collectives and lax.ppermute only.
A program may use at most 64 MiB of HBM per device.

v0:
```python
import jax
import jax.numpy as jnp
from jax import lax
from jax.sharding import PartitionSpec as P

C = 1000
BLOCK = 128


def body(documents, landmarks, eigen_vectors, land_degree, eigen_values, tile_mask, labels):
    inverse_width = 4.0 / documents.shape[1]
    land_rows = landmarks.shape[0]
    col_index = lax.axis_index("col")
    col_count = lax.axis_size("col")
    scaled = (
        eigen_vectors.astype(jnp.float32) * lax.rsqrt(land_degree)[:, None] / eigen_values[None, :]
    ).astype(jnp.bfloat16)
    doc_square = jnp.sum(jnp.square(documents.astype(jnp.float32)), 1)
    land_piece = lax.all_gather(landmarks, "blk", axis=0, tiled=True)
    vector_piece = lax.all_gather(scaled, "blk", axis=0, tiled=True)
    piece_rows = land_piece.shape[0]
    offsets = jnp.arange(piece_rows, dtype=jnp.int32)
    whole_rows = (
        offsets // land_rows * (land_rows * col_count) + col_index * land_rows + offsets % land_rows
    )
    live_cols = jnp.take(tile_mask, whole_rows // BLOCK, axis=1)
    land_square = jnp.sum(jnp.square(land_piece.astype(jnp.float32)), 1)
    products = jnp.einsum("df,lf->dl", documents, land_piece, preferred_element_type=jnp.float32)
    keep = jnp.repeat(live_cols, BLOCK, axis=0).astype(jnp.float32)
    weights = (
        jnp.exp(inverse_width * (2.0 * products - doc_square[:, None] - land_square[None, :]))
        * keep
    )
    total = jnp.dot(weights.astype(jnp.bfloat16), vector_piece, preferred_element_type=jnp.float32)
    projection = total
    degree = jnp.sum(weights, 1)
    projection, degree = (
        lax.psum_scatter(projection, "col", scatter_dimension=0, tiled=True),
        lax.psum_scatter(degree, "col", scatter_dimension=0, tiled=True),
    )
    embedding = projection * lax.rsqrt(degree)[:, None]
    unit_rows = embedding * lax.rsqrt(jnp.sum(jnp.square(embedding), 1, keepdims=True) + 1e-06)
    one_hot = (jnp.arange(C, dtype=jnp.int32)[:, None] == labels[None, :]).astype(jnp.float32)
    partial_sums = jnp.dot(
        one_hot, unit_rows, precision=lax.Precision.HIGHEST, preferred_element_type=jnp.float32
    )
    centroids = lax.psum(partial_sums, ("blk", "col"))
    return (embedding, centroids)


def solution(mesh):
    placed = (
        P("blk", None),
        P(("blk", "col"), None),
        P(("blk", "col"), None),
        P(("blk", "col")),
        P(),
        P("blk", None),
        P(("blk", "col")),
    )
    return jax.shard_map(
        body, mesh=mesh, in_specs=placed, out_specs=(P(("blk", "col"), None), P()), check_vma=False
    )
```

profile of v0, /device:TPU:0, one launch (start us, length us, event | category | flops | bytes accessed | tf_op | source)
XLA Modules:
  0.0 211.5 jit_solution(13693534554832711578)
XLA Ops:
  7.2 0.0 all-gather.2.cloned.1.call-start
  7.2 0.7 all-gather.2.cloned.1.call-update
  7.9 0.0 reduce-scatter.2.cloned.1.call-start
  8.0 0.8 copy.13
  8.8 2.8 %gather_fusion = s32[1024,6]{1,0:T(8,128)S(1)} fusion(s32[6,32]{0,1:T(8,128)S(1)} %copy.13, s32[1024]{0:T(1024)S(1)} %broadcast_clamp_fusion), kind=kCustom, calls=%fused_computation | custom fusion | bytes 53248 | tf_op jit(solution)/shard_map/jit(_take)/gather | solution.py:26
  11.7 0.2 convert_bitcast_fusion
  11.9 0.2 copy.14
  12.1 0.0 copy-done.4
  12.1 0.0 copy-done.3
  12.1 0.1 divide_convert_fusion
  12.2 11.3 %all_gather.7 = bf16[1024,256]{1,0:T(8,128)(2,1)S(1)} all-gather(bf16[128,256]{1,0:T(8,128)(2,1)S(1)} %divide_convert_fusion), channel_id=1, replica_groups=mesh['blk'=8,'col'=4] {'blk'}, dimensions={0}, use_global_device_ids=true | all-gather | bytes 589824 | tf_op jit(solution)/shard_map/all_gather | solution.py:20
  23.5 0.0 copy-done.1
  23.5 0.3 multiply_reduce_fusion.1
  23.8 14.6 %all-gather.2.cloned.1.call-done = bf16[1024,768]{1,0:T(8,128)(2,1)} async-done(((bf16[128,768]{1,0:T(8,128)(2,1)}), bf16[1024,768]{1,0:T(8,128)(2,1)}) %all-gather.2.cloned.1.call-update) | async-done | bytes 1572880 | tf_op jit(solution)/shard_map/all_gather | solution.py:19
  38.4 1.9 multiply_reduce_fusion
  40.3 1.8 fusion
  42.1 0.0 copy-start.7
  42.1 0.0 copy-start.5
  42.1 1.5 fusion.21
  43.6 0.0 reduce-scatter.2.cloned.1.call-update
  43.6 0.0 all-reduce.3.cloned.1.call-start
  43.7 0.6 dynamic-slice
  44.9 12.0 %all-reduce = f32[768]{0:T(1024)S(1)} all-reduce(f32[768]{0:T(1024)S(1)} %get-tuple-element.4), channel_id=3, replica_groups=mesh['blk'=8,'col'=4] {'col'}, use_global_device_ids=true, to_apply=%region_4.5.clone | all-reduce | flops 768 | bytes 6144
  56.9 0.1 dynamic-slice_rsqrt_fusion
  57.0 10.1 %reduce-scatter.2.cloned.1.call-done = f32[192,256]{1,0:T(8,128)} async-done(((f32[768,256]{1,0:T(8,128)}), f32[192,256]{1,0:T(8,128)}) %reduce-scatter.2.cloned.1.call-update) | async-done | bytes 196624 | tf_op jit(solution)/shard_map/reduce_scatter | solution.py:38
  67.1 1.1 multiply_reduce_fusion.2
  68.2 0.0 copy-start.2
  68.2 0.0 copy-done.5
  68.2 1.6 fusion.2
  69.9 0.0 all-reduce.3.cloned.1.call-update
  69.9 132.8 %all-reduce.3.cloned.1.call-done = f32[1000,256]{1,0:T(8,128)} async-done(((f32[1000,256]{1,0:T(8,128)}), f32[1000,256]{1,0:T(8,128)}) %all-reduce.3.cloned.1.call-update) | async-done | bytes 1024016 | tf_op jit(solution)/shard_map/psum | solution.py:47
  202.7 2.2 %copy.16 = f32[1000,256]{1,0:T(8,128)} copy(f32[1000,256]{1,0:T(8,128)} %all-reduce.3.cloned.1.call-done) | data formatting | bytes 2048000
  (14 shorter events, 0.1 us)
Async XLA Ops:
  7.2 4.9 %copy-start.6 = (f32[128]{0:T(128)S(1)}, f32[128]{0:T(128)}, u32[]{:S(2)}) copy-start(f32[128]{0:T(128)} %param.10) | copy-start | bytes 1540
  7.2 4.9 %copy-start.4 = (f32[256]{0:T(256)S(1)}, f32[256]{0:T(256)}, u32[]{:S(2)}) copy-start(f32[256]{0:T(256)} %param.11) | copy-start | bytes 3076
  7.2 4.9 %copy-start.3 = (bf16[128,256]{1,0:T(8,128)(2,1)S(1)}, bf16[128,256]{1,0:T(8,128)(2,1)}, u32[]{:S(2)}) copy-start(bf16[128,256]{1,0:T(8,128)(2,1)} %param.9) | copy-start | bytes 196612
  7.2 16.3 %copy-start.1 = (bf16[768,768]{1,0:T(8,128)(2,1)S(1)}, bf16[768,768]{1,0:T(8,128)(2,1)}, u32[]{:S(2)}) copy-start(bf16[768,768]{1,0:T(8,128)(2,1)} %param.7) | copy-start | bytes 3538948
  7.2 31.2 %all-gather.2.cloned.1.call-start = ((), (), s32[]{:S(2)}) async-start(), calls=%async_computation.1 | async-start | bytes 1769472 | tf_op jit(solution)/shard_map/all_gather | solution.py:19
  7.9 59.2 %reduce-scatter.2.cloned.1.call-start = ((), (), s32[]{:S(2)}) async-start(), calls=%async_computation.2 | async-start | bytes 983040 | tf_op jit(solution)/shard_map/reduce_scatter | solution.py:38
  38.4 1.9 copy-start
  42.1 1.6 copy-start.7
  42.1 26.1 %copy-start.5 = (s32[192]{0:T(256)S(1)}, s32[192]{0:T(256)}, u32[]{:S(2)}) copy-start(s32[192]{0:T(256)} %param.13) | copy-start | bytes 2308
  43.6 159.1 %all-reduce.3.cloned.1.call-start = ((), (), s32[]{:S(2)}) async-start(), calls=%async_computation.3 | async-start | bytes 2048000 | tf_op jit(solution)/shard_map/psum | solution.py:47
  68.2 136.8 %copy-start.2 = (f32[192,256]{1,0:T(8,128)}, f32[192,256]{1,0:T(8,128)S(1)}, u32[]{:S(2)}) copy-start(f32[192,256]{1,0:T(8,128)S(1)} %get-tuple-element.6) | copy-start | bytes 589828
Sparse Core Ops, SparseCore 0:
  9.9 28.4 all-gather.1
  43.8 23.2 reduce-scatter.1
  72.8 129.8 all-reduce.2
where the time goes:
time: 212 us
  waiting for transfers between devices  158 us (75%)
  blocking collectives  23.3 us (11%)
  between operations  14.6 us (7%)
  local copies, waits for them, and re-layouts  6.71 us (3%)
  matrix products  4.9 us (2%)
  other arithmetic  3.66 us (2%)
    psum x1, waiting for transfers between devices, body(): centroids = lax.psum(partial_sums, ('blk', 'col'))  133 us
    all_gather x1, waiting for transfers between devices, body(): land_piece = lax.all_gather(landmarks, 'blk', axis=0, tiled=True)  14.6 us
    unnamed x1, blocking collectives  12 us
    all_gather x1, blocking collectives, body(): vector_piece = lax.all_gather(scaled, 'blk', axis=0, tiled=True)  11.3 us
    reduce_scatter x1, waiting for transfers between devices, body(): lax.psum_scatter(projection, 'col', scatter_dimension=0, tiled=True)  10.1 us
  transfers between devices with their start and end apart: 3, of which 3 were waited for; matrix products, arithmetic and copies ran while one was open for 2% of the time, Pallas kernels for 0%

commit v1 on v0

--- a/solution.py
+++ b/solution.py
@@ -16,8 +16,11 @@
         eigen_vectors.astype(jnp.float32) * lax.rsqrt(land_degree)[:, None] / eigen_values[None, :]
     ).astype(jnp.bfloat16)
     doc_square = jnp.sum(jnp.square(documents.astype(jnp.float32)), 1)
-    land_piece = lax.all_gather(landmarks, "blk", axis=0, tiled=True)
-    vector_piece = lax.all_gather(scaled, "blk", axis=0, tiled=True)
+    land_piece, vector_piece = jnp.split(
+        lax.all_gather(jnp.concatenate([landmarks, scaled], axis=1), "blk", axis=0, tiled=True),
+        [landmarks.shape[1]],
+        axis=1,
+    )
     piece_rows = land_piece.shape[0]
     offsets = jnp.arange(piece_rows, dtype=jnp.int32)
     whole_rows = (

time: 212 us -> 218 us (1.028)
  blocking collectives: 23.3 us -> 12 us
  waiting for transfers between devices: 158 us -> 165 us
  other arithmetic: 3.66 us -> 7.41 us
  matrix products: 4.9 us -> 8.3 us
  local copies, waits for them, and re-layouts: 6.71 us -> 10.1 us
    all_gather x1 -> x0, blocking collectives: 11.3 us -> none  [body(): vector_piece = lax.all_gather(scaled, 'blk', axis=0, tiled=True)]
    all_gather x1, waiting for transfers between devices: 14.6 us -> 22.1 us  [body(): lax.all_gather(jnp.concatenate([landmarks, scaled], axis=1), 'blk', axis=...]
    convert_element_type x1 -> x2, local copies, waits for them, and re-layouts: 0.19 us -> 2.55 us  [body(): keep = jnp.repeat(live_cols, BLOCK, axis=0).astype(jnp.float32)]
    dot_general x1, matrix products: 1.8 us -> 4.12 us  [body(): jnp.einsum('df,lf->dl', documents, land_piece, preferred_element_type=jnp...]
  transfers between devices with their start and end apart: 3 -> 3, of which waited for: 3 -> 3; matrix products, arithmetic and copies ran while one was open for 2% -> 4% of each run, Pallas kernels for 0% -> 0%
where the time goes in v1:
time: 218 us
  waiting for transfers between devices  165 us (76%)
  between operations  14.5 us (7%)
  blocking collectives  12 us (6%)
  local copies, waits for them, and re-layouts  10.1 us (5%)
  matrix products  8.3 us (4%)
  other arithmetic  7.41 us (3%)
    psum x1, waiting for transfers between devices, body(): centroids = lax.psum(partial_sums, ('blk', 'col'))  133 us
    all_gather x1, waiting for transfers between devices, body(): lax.all_gather(jnp.concatenate([landmarks, scaled], axis=1), 'blk', axis=...  22.1 us
    unnamed x1, blocking collectives  12 us
    reduce_scatter x1, waiting for transfers between devices, body(): lax.psum_scatter(projection, 'col', scatter_dimension=0, tiled=True)  10 us
  transfers between devices with their start and end apart: 3, of which 3 were waited for; matrix products, arithmetic and copies ran while one was open for 4% of the time, Pallas kernels for 0%

profile of v1, /device:TPU:0, one launch (start us, length us, event | category | flops | bytes accessed | tf_op | source)
XLA Modules:
  0.0 217.5 jit_solution(15986826658632600904)
XLA Ops:
  7.2 0.0 all-gather.2.cloned.1.call-start
  7.2 0.7 rsqrt.14
  7.9 0.9 divide_convert_fusion
  8.8 1.7 pad_maximum_fusion
  10.5 0.0 all-gather.2.cloned.1.call-update
  10.5 0.0 reduce-scatter.2.cloned.1.call-start
  10.5 0.8 copy.13
  11.4 2.8 %gather_fusion = s32[1024,6]{1,0:T(8,128)S(1)} fusion(s32[6,32]{0,1:T(8,128)S(1)} %copy.13, s32[1024]{0:T(1024)S(1)} %broadcast_clamp_fusion), kind=kCustom, calls=%fused_computation | custom fusion | bytes 53248 | tf_op jit(solution)/shard_map/jit(_take)/gather | solution.py:29
  14.2 0.2 convert_bitcast_fusion
  14.4 0.2 copy.14
  14.6 0.4 broadcast_in_dim.14
  15.0 2.4 %copy.15 = f32[768,1024]{0,1:T(8,128)} copy(f32[768,1024]{1,0:T(8,128)S(1)} %bitcast.9) | data formatting | bytes 6291456 | tf_op jit(solution)/shard_map/convert_element_type | solution.py:32
  17.4 1.7 multiply_reduce_fusion.1
  19.0 22.1 %all-gather.2.cloned.1.call-done = bf16[1024,1024]{1,0:T(8,128)(2,1)} async-done(((bf16[128,1024]{1,0:T(8,128)(2,1)}), bf16[1024,1024]{1,0:T(8,128)(2,1)}) %all-gather.2.cloned.1.call-update) | async-done | bytes 2097168 | tf_op jit(solution)/shard_map/all_gather | solution.py:20
  41.1 1.8 multiply_reduce_fusion
  42.9 0.0 copy-done
  42.9 4.1 %fusion.23 = (f32[768]{0:T(1024)S(1)}, bf16[768,1024]{0,1:T(8,128)(2,1)S(1)}) fusion(f32[768,1024]{0,1:T(8,128)} %copy.15, f32[1024]{0:T(1024)S(1)} %multiply_reduce_fusion, f32[768]{0:T(1024)S(1)} %multiply_reduce_fusion.1, bf16[768,768]{1,0:T(8,128)(2,1)S(1)} %copy-done, bf16[1024,1024]{1,0:T(8,128)(2,1)} %all-gather.2.cloned.1.call-done), kind=kOutput, calls=%fused_computation.57 | convolution fusion | flops 1213463808 | bytes 7481344 | tf_op jit(solution)/shard_map/df,lf->dl/dot_general | solution.py:31
  47.1 0.0 copy-start.3
  47.1 0.0 copy-start.2
  47.1 2.5 %fusion = f32[768,256]{1,0:T(8,128)} fusion(bf16[768,1024]{0,1:T(8,128)(2,1)S(1)} %get-tuple-element.5, bf16[1024,1024]{1,0:T(8,128)(2,1)} %all-gather.2.cloned.1.call-done), kind=kOutput, calls=%fused_computation.4 | convolution fusion | flops 402653184 | bytes 2883584 | tf_op jit(solution)/shard_map/dot_general | solution.py:37
  49.6 0.0 reduce-scatter.2.cloned.1.call-update
  49.7 0.0 all-reduce.3.cloned.1.call-start
  49.7 0.6 dynamic-slice
  51.0 12.0 %all-reduce = f32[768]{0:T(1024)S(1)} all-reduce(f32[768]{0:T(1024)S(1)} %get-tuple-element.4), channel_id=3, replica_groups=mesh['blk'=8,'col'=4] {'col'}, use_global_device_ids=true, to_apply=%region_4.5.clone | all-reduce | flops 768 | bytes 6144
  63.0 0.1 dynamic-slice_rsqrt_fusion
  63.1 10.0 %reduce-scatter.2.cloned.1.call-done = f32[192,256]{1,0:T(8,128)} async-done(((f32[768,256]{1,0:T(8,128)}), f32[192,256]{1,0:T(8,128)}) %reduce-scatter.2.cloned.1.call-update) | async-done | bytes 196624 | tf_op jit(solution)/shard_map/reduce_scatter | solution.py:41
  73.1 1.1 multiply_reduce_fusion.2
  74.2 0.0 copy-start.1
  74.2 1.6 fusion.3
  75.9 0.0 all-reduce.3.cloned.1.call-update
  75.9 132.8 %all-reduce.3.cloned.1.call-done = f32[1000,256]{1,0:T(8,128)} async-done(((f32[1000,256]{1,0:T(8,128)}), f32[1000,256]{1,0:T(8,128)}) %all-reduce.3.cloned.1.call-update) | async-done | bytes 1024016 | tf_op jit(solution)/shard_map/psum | solution.py:50
  208.7 2.2 %copy.17 = f32[1000,256]{1,0:T(8,128)} copy(f32[1000,256]{1,0:T(8,128)} %all-reduce.3.cloned.1.call-done) | data formatting | bytes 2048000
  (8 shorter events, 0.1 us)
Async XLA Ops:
  7.2 34.0 %all-gather.2.cloned.1.call-start = ((), (), s32[]{:S(2)}) async-start(), calls=%async_computation.1 | async-start | bytes 2359296 | tf_op jit(solution)/shard_map/all_gather | solution.py:20
  10.5 62.6 %reduce-scatter.2.cloned.1.call-start = ((), (), s32[]{:S(2)}) async-start(), calls=%async_computation.2 | async-start | bytes 983040 | tf_op jit(solution)/shard_map/reduce_scatter | solution.py:41
  17.4 25.6 %copy-start = (bf16[768,768]{1,0:T(8,128)(2,1)S(1)}, bf16[768,768]{1,0:T(8,128)(2,1)}, u32[]{:S(2)}) copy-start(bf16[768,768]{1,0:T(8,128)(2,1)} %param.7) | copy-start | bytes 3538948
  47.1 2.6 %copy-start.3 = (u32[32]{0:T(128)S(1)}, u32[32]{0:T(128)}, u32[]{:S(2)}) copy-start(u32[32]{0:T(128)} %constant.75) | copy-start | bytes 388
  47.1 27.1 %copy-start.2 = (s32[192]{0:T(256)S(1)}, s32[192]{0:T(256)}, u32[]{:S(2)}) copy-start(s32[192]{0:T(256)} %param.13) | copy-start | bytes 2308
  49.7 159.1 %all-reduce.3.cloned.1.call-start = ((), (), s32[]{:S(2)}) async-start(), calls=%async_computation.3 | async-start | bytes 2048000 | tf_op jit(solution)/shard_map/psum | solution.py:50
  74.2 136.8 %copy-start.1 = (f32[192,256]{1,0:T(8,128)}, f32[192,256]{1,0:T(8,128)S(1)}, u32[]{:S(2)}) copy-start(f32[192,256]{1,0:T(8,128)S(1)} %get-tuple-element.8) | copy-start | bytes 589828
Sparse Core Ops, SparseCore 0:
  10.6 30.4 all-gather.1
  49.8 23.2 reduce-scatter.1
  78.8 129.8 all-reduce.2
